TPU v7x, 32 devices: a whole 2x2x4 slice. The times are simulated.
32 devices in a mesh: rep: 2 (over x), node: 8 (over z, y), local: 2 (over core).
Axes of the slice: x: 2, y: 2, z: 4, core: 2. Of those that a mesh axis runs over, the one named last changes fastest.
Arguments:
- tokens: bfloat16 [2048, 7168], P(('rep', 'node', 'local')), parts along dimension 0, may hold values from -6 to 6
- gate_ids: int32 [2048, 4], P(('rep', 'node', 'local')), parts along dimension 0, may hold values from 0 to 7, all different within a row; in each aligned block of 64 rows (0 to 63, 64 to 127, ...) at most 64 rows name the same one
- gate_values: bfloat16 [2048, 4], P(('rep', 'node', 'local')), parts along dimension 0, may hold values from 0.049804688 to 1
- w_gate: bfloat16 [8, 7168, 1024], P('node', None, 'local'), may hold values from -0.0625 to 0.0625
- w_up: bfloat16 [8, 7168, 1024], P('node', None, 'local'), may hold values from -0.0625 to 0.0625
- w_down: bfloat16 [8, 1024, 7168], P('node', 'local'), may hold values from -0.1875 to 0.1875
Outputs:
- mixed: bfloat16 [2048, 7168], P(('rep', 'node', 'local')), parts along dimension 0
There are 2 independent parts, one for each index of `rep`. A program takes and returns all parts, laid end to end along the dimension named above; an argument that names none is the same for every part. Nothing has to cross between parts.
Inputs may be any that keep to these rules, and one draw needn't show every extreme that they name: `gate_ids`: each row names 4 different experts. Within the rows of one device, no expert is named by more than 64 rows, and in every draw some expert is named by exactly 64 rows of some device.
All inputs are finite; a program needn't handle non-finite values.
Results may differ from a plain program's by a relative error of at most 0.0065.
Values may be sent and summed in bfloat16 or wider, within the bound.
A program may use at most 128 MiB of HBM per device.

v0:
```python
import jax
import jax.numpy as jnp
from jax import lax
from jax.sharding import PartitionSpec as P


def per_device(tokens, gate_ids, gate_values, w_gate, w_up, w_down):
    node_count = lax.axis_size("node")
    token_count = tokens.shape[0]
    choose_count = gate_ids.shape[1]
    width = tokens.shape[1]
    capacity = 2 * token_count * choose_count // node_count
    flat_ids = gate_ids.reshape(-1)
    expert_row = jnp.arange(node_count, dtype=jnp.int32)
    onehot = (flat_ids[:, None] == expert_row[None, :]).astype(jnp.int32)
    earlier = jnp.cumsum(onehot, axis=0) - onehot
    within = jnp.sum(earlier * onehot, axis=1)
    slot = (flat_ids * capacity + within).reshape(token_count, choose_count)
    slot_row = jnp.arange(node_count * capacity, dtype=jnp.int32)
    matches = slot[:, :, None] == slot_row[None, None, :]
    select = jnp.any(matches, axis=1).astype(jnp.bfloat16)
    combine_table = jnp.sum(
        jnp.where(matches, gate_values.astype(jnp.float32)[:, :, None], jnp.float32(0.0)), axis=1
    ).astype(jnp.bfloat16)
    outgoing = jnp.einsum("ts,td->sd", select, tokens, preferred_element_type=jnp.float32).astype(
        jnp.bfloat16
    )
    outgoing = outgoing.reshape(node_count, capacity, width)
    gathered = lax.all_gather(
        lax.all_to_all(outgoing, "node", split_axis=0, concat_axis=0, tiled=True),
        "local",
        axis=0,
        tiled=True,
    )
    rows = gathered.reshape(-1, width)
    gate_act = jnp.dot(rows, w_gate[0], preferred_element_type=jnp.float32)
    up_act = jnp.dot(rows, w_up[0], preferred_element_type=jnp.float32)
    hidden = (jax.nn.silu(gate_act) * up_act).astype(jnp.bfloat16)
    partial_value = (
        jnp.dot(hidden, w_down[0], preferred_element_type=jnp.float32)
        .astype(jnp.bfloat16)
        .reshape(gathered.shape)
    )
    partial_value = lax.optimization_barrier(partial_value).astype(jnp.float32)
    own_rows = lax.psum_scatter(
        partial_value.astype(jnp.bfloat16), "local", scatter_dimension=0, tiled=True
    )
    expert_out = lax.all_to_all(own_rows, "node", split_axis=0, concat_axis=0, tiled=True)
    result = jnp.dot(
        combine_table,
        expert_out.reshape(node_count * capacity, width),
        preferred_element_type=jnp.float32,
    )
    return result.astype(jnp.bfloat16)


def solution(mesh):
    return jax.shard_map(
        per_device,
        mesh=mesh,
        in_specs=(
            P(("rep", "node", "local"), None),
            P(("rep", "node", "local"), None),
            P(("rep", "node", "local"), None),
            P("node", None, "local"),
            P("node", None, "local"),
            P("node", "local", None),
        ),
        out_specs=P(("rep", "node", "local"), None),
        check_vma=False,
    )
```

profile of v0, /device:TPU:0, one launch (start us, length us, event | category | flops | bytes accessed | tf_op | source)
XLA Modules:
  0.0 445.9 jit_solution(14984800012365417282)
XLA Ops:
  6.5 0.0 copy-start
  6.5 0.0 all-gather.2.cloned.1.call-start
  6.5 0.9 copy.24
  7.4 0.1 eq.42
  7.5 0.1 eq.38
  7.6 0.6 reduce-window.6
  8.2 0.2 slice_reduce_fusion
  8.5 0.1 fusion.10
  8.6 0.1 reduce_sum.21
  8.7 0.1 copy.26
  8.7 0.7 multiply_add_fusion
  9.4 0.1 fusion.7
  9.6 0.0 copy-done
  9.6 2.1 convolution_convert_fusion.1
  11.7 167.8 %all_to_all.10 = bf16[8,64,7168]{2,1,0:T(8,128)(2,1)} all-to-all(bf16[8,64,7168]{2,1,0:T(8,128)(2,1)S(1)} %bitcast.30), channel_id=1, replica_groups=mesh['rep'=2,'node'=8,'local'=2] {'node'}, dimensions={0} | all-to-all | bytes 14680064 | tf_op jit(solution)/shard_map/all_to_all | solution.py:30
  179.5 0.0 all-gather.2.cloned.1.call-update
  179.5 0.0 reduce-scatter.2.cloned.1.call-start
  179.6 26.1 %all-gather.2.cloned.1.call-done = bf16[16,64,7168]{2,1,0:T(8,128)(2,1)} async-done(((bf16[8,64,7168]{2,1,0:T(8,128)(2,1)}), bf16[16,64,7168]{2,1,0:T(8,128)(2,1)}) %all-gather.2.cloned.1.call-update) | async-done | bytes 14680080 | tf_op jit(solution)/shard_map/all_gather | solution.py:29
  205.7 0.0 copy-start.3
  205.7 0.0 slice-start
  205.7 13.4 %fusion.1 = f32[1024,512]{1,0:T(8,128)S(1)} fusion(bf16[1024,7168]{1,0:T(8,128)(2,1)} %bitcast.32, bf16[1,7168,512]{2,1,0:T(8,128)(2,1)} %param.10), kind=kOutput, calls=%fused_computation.4 | convolution fusion | flops 7516192768 | bytes 24117248 | tf_op jit(solution)/shard_map/dot_general | solution.py:37
  219.1 0.0 copy-done.3
  219.1 0.0 slice-start.1
  219.1 10.3 %multiply_convert_fusion = bf16[1024,512]{1,0:T(8,128)(2,1)S(1)} fusion(f32[1024,512]{1,0:T(8,128)S(1)} %fusion.1, bf16[1024,7168]{1,0:T(8,128)(2,1)S(1)} %bitcast.33, bf16[1,7168,512]{2,1,0:T(8,128)(2,1)} %param.9), kind=kOutput, calls=%fused_computation.8 | convolution fusion | flops 7519338496 | bytes 25165824 | tf_op jit(solution)/shard_map/dot_general | solution.py:36
  229.4 0.0 slice-done
  229.4 0.0 slice-done.1
  229.4 11.1 %convolution_convert_fusion = bf16[1024,7168]{1,0:T(8,128)(2,1)} fusion(bf16[1024,512]{1,0:T(8,128)(2,1)S(1)} %multiply_convert_fusion, bf16[1,512,7168]{2,1,0:T(8,128)(2,1)S(1)} %bitcast.35), kind=kOutput, calls=%fused_computation | convolution fusion | flops 7523532800 | bytes 23068672 | tf_op jit(solution)/shard_map/dot_general | solution.py:40
  240.5 0.0 reduce-scatter.2.cloned.1.call-update
  240.5 0.0 copy-start.2
  240.5 26.1 %reduce-scatter.2.cloned.1.call-done = bf16[8,64,7168]{2,1,0:T(8,128)(2,1)} async-done(((bf16[16,64,7168]{2,1,0:T(8,128)(2,1)}), bf16[8,64,7168]{2,1,0:T(8,128)(2,1)}) %reduce-scatter.2.cloned.1.call-update) | async-done | bytes 7340048 | tf_op jit(solution)/shard_map/reduce_scatter | solution.py:45
  266.7 5.9 %all-to-all-start.1 = ((bf16[8,64,7168]{2,1,0:T(8,128)(2,1)}), bf16[8,64,7168]{2,1,0:T(8,128)(2,1)}, u32[]{:S(2)}, u32[]{:S(2)}) async-start(bf16[8,64,7168]{2,1,0:T(8,128)(2,1)} %reduce-scatter.2.cloned.1.call-done), calls=%async_computation.2 | async-start | bytes 14680064 | tf_op jit(solution)/shard_map/all_to_all | solution.py:48
  272.6 0.0 copy-done.2
  272.6 0.0 copy-start.1
  272.6 0.1 select_reduce_fusion
  272.7 160.8 %all-to-all-done.1 = bf16[8,64,7168]{2,1,0:T(8,128)(2,1)} async-done(((bf16[8,64,7168]{2,1,0:T(8,128)(2,1)}), bf16[8,64,7168]{2,1,0:T(8,128)(2,1)}, u32[]{:S(2)}, u32[]{:S(2)}) %all-to-all-start.1) | async-done | bytes 7340064 | tf_op jit(solution)/shard_map/all_to_all | solution.py:48
  433.6 5.4 %convolution_convert_fusion.2 = bf16[64,7168]{1,0:T(8,128)(2,1)} fusion(bf16[512,7168]{1,0:T(8,128)(2,1)} %bitcast.8, bf16[64,512]{1,0:T(8,128)(2,1)S(1)} %select_reduce_fusion), kind=kOutput, calls=%fused_computation.2 | convolution fusion | flops 470220800 | bytes 8323072 | tf_op jit(solution)/shard_map/dot_general | solution.py:49
  439.0 0.0 copy-done.1
  (5 shorter events, 0.1 us)
Async XLA Ops:
  6.5 3.1 copy-start
  6.5 199.2 %all-gather.2.cloned.1.call-start = ((), (), s32[]{:S(2)}) async-start(), calls=%async_computation.3 | async-start | bytes 22020096 | tf_op jit(solution)/shard_map/all_gather | solution.py:29
  179.5 87.1 %reduce-scatter.2.cloned.1.call-start = ((), (), s32[]{:S(2)}) async-start(), calls=%async_computation.4 | async-start | bytes 22020096 | tf_op jit(solution)/shard_map/reduce_scatter | solution.py:45
  205.7 13.4 %copy-start.3 = (bf16[16,64,7168]{2,1,0:T(8,128)(2,1)S(1)}, bf16[16,64,7168]{2,1,0:T(8,128)(2,1)}, u32[]{:S(2)}) copy-start(bf16[16,64,7168]{2,1,0:T(8,128)(2,1)} %all-gather.2.cloned.1.call-done) | copy-start | bytes 44040196
  205.7 23.7 %slice-start = ((s8[7340032]{0:T(1024)(128)(4,1)}), s8[4194304]{0:T(1024)(128)(4,1)S(1)}, s32[]{:S(2)}) async-start(s8[7340032]{0:T(1024)(128)(4,1)} %bitcast.34), calls=%async_computation.5 | async-start | bytes 8388608
  219.1 10.3 %slice-start.1 = ((s8[7340032]{0:T(1024)(128)(4,1)}), s8[3145728]{0:T(1024)(128)(4,1)S(1)}, s32[]{:S(2)}) async-start(s8[7340032]{0:T(1024)(128)(4,1)} %bitcast.34), calls=%async_computation.6 | async-start | bytes 6291456
  240.5 32.1 %copy-start.2 = (bf16[64,4]{0,1:T(4,128)(2,1)S(1)}, bf16[64,4]{0,1:T(4,128)(2,1)}, u32[]{:S(2)}) copy-start(bf16[64,4]{0,1:T(4,128)(2,1)} %param.8) | copy-start | bytes 1540
  266.7 166.9 %all-to-all-start.1 = ((bf16[8,64,7168]{2,1,0:T(8,128)(2,1)}), bf16[8,64,7168]{2,1,0:T(8,128)(2,1)}, u32[]{:S(2)}, u32[]{:S(2)}) async-start(bf16[8,64,7168]{2,1,0:T(8,128)(2,1)} %reduce-scatter.2.cloned.1.call-done), calls=%async_computation.2 | async-start | bytes 14680064 | tf_op jit(solution)/shard_map/all_to_all | solution.py:48
  272.6 166.4 %copy-start.1 = (bf16[64,7168]{1,0:T(8,128)(2,1)S(1)}, bf16[64,7168]{1,0:T(8,128)(2,1)}, u32[]{:S(2)}) copy-start(bf16[64,7168]{1,0:T(8,128)(2,1)} %param.6) | copy-start | bytes 2752516
Sparse Core Ops, SparseCore 0:
  179.7 26.0 all-gather.1
  240.6 25.9 reduce-scatter.1
where the time goes:
time: 446 us
  waiting for transfers between devices  213 us (48%)
  blocking collectives  168 us (38%)
  matrix products  42.2 us (9%)
  between operations  13.5 us (3%)
  starting transfers between devices  5.94 us (1%)
    all_to_all x1, blocking collectives, per_device(): lax.all_to_all(outgoing, 'node', split_axis=0, concat_axis=0, tiled=True)  168 us
    all_to_all x1, waiting for transfers between devices, per_device(): lax.all_to_all(own_rows, 'node', split_axis=0, concat_axis=0, tiled=True)  161 us
    reduce_scatter x1, waiting for transfers between devices, per_device(): lax.psum_scatter(partial_value.astype(jnp.bfloat16), 'local', scatter_dim...  26.1 us
    all_gather x1, waiting for transfers between devices, per_device(): lax.all_gather(lax.all_to_all(outgoing, 'node', split_axis=0, concat_axis...  26.1 us
    dot_general x1, matrix products, per_device(): up_act = jnp.dot(rows, w_up[0], preferred_element_type=jnp.float32)  13.4 us
    dot_general x1, matrix products, per_device(): jnp.dot(hidden, w_down[0], preferred_element_type=jnp.float32)  11.1 us
    dot_general x1, matrix products, per_device(): gate_act = jnp.dot(rows, w_gate[0], preferred_element_type=jnp.float32)  10.3 us
  transfers between devices with their start and end apart: 3, of which 3 were waited for; matrix products, arithmetic and copies ran while one was open for 0% of the time, Pallas kernels for 0%

commit v1 on v0

--- a/solution.py
+++ b/solution.py
@@ -26,11 +26,17 @@
         jnp.bfloat16
     )
     outgoing = outgoing.reshape(node_count, capacity, width)
-    gathered = lax.all_gather(
-        lax.all_to_all(outgoing, "node", split_axis=0, concat_axis=0, tiled=True),
-        "local",
+    gathered = jnp.concatenate(
+        lax.all_to_all(
+            jnp.stack(
+                [lax.all_to_all(outgoing, "node", split_axis=0, concat_axis=0, tiled=True)]
+                * lax.axis_size("local")
+            ),
+            "local",
+            0,
+            0,
+        ),
         axis=0,
-        tiled=True,
     )
     rows = gathered.reshape(-1, width)
     gate_act = jnp.dot(rows, w_gate[0], preferred_element_type=jnp.float32)

time: 446 us -> 432 us (0.969)
  waiting for transfers between devices: 213 us -> 185 us
  blocking collectives: 168 us -> 183 us
    all_gather x1 -> x0, waiting for transfers between devices: 26.1 us -> none  [per_device(): lax.all_gather(lax.all_to_all(outgoing, 'node', split_axis=0, concat_axis...]
    all_to_all x0 -> x1, blocking collectives: none -> 15.8 us  [per_device(): lax.all_to_all(jnp.stack([lax.all_to_all(outgoing, 'node', split_axis=0,...]
    dot_general x1, matrix products: 13.4 us -> 7.71 us  [per_device(): up_act = jnp.dot(rows, w_up[0], preferred_element_type=jnp.float32)]
  transfers between devices with their start and end apart: 3 -> 2, of which waited for: 3 -> 2; matrix products, arithmetic and copies ran while one was open for 0% -> 0% of each run, Pallas kernels for 0% -> 0%
where the time goes in v1:
time: 432 us
  waiting for transfers between devices  185 us (43%)
  blocking collectives  183 us (42%)
  matrix products  39.4 us (9%)
  between operations  13.5 us (3%)
  starting transfers between devices  5.91 us (1%)
    all_to_all x1, blocking collectives, per_device(): lax.all_to_all(outgoing, 'node', split_axis=0, concat_axis=0, tiled=True)  168 us
    all_to_all x1, waiting for transfers between devices, per_device(): lax.all_to_all(own_rows, 'node', split_axis=0, concat_axis=0, tiled=True)  161 us
    reduce_scatter x1, waiting for transfers between devices, per_device(): lax.psum_scatter(partial_value.astype(jnp.bfloat16), 'local', scatter_dim...  24 us
    all_to_all x1, blocking collectives, per_device(): lax.all_to_all(jnp.stack([lax.all_to_all(outgoing, 'node', split_axis=0,...  15.8 us
    dot_general x1, matrix products, per_device(): jnp.dot(hidden, w_down[0], preferred_element_type=jnp.float32)  14.1 us
    dot_general x1, matrix products, per_device(): gate_act = jnp.dot(rows, w_gate[0], preferred_element_type=jnp.float32)  10.1 us
  transfers between devices with their start and end apart: 2, of which 2 were waited for; matrix products, arithmetic and copies ran while one was open for 0% of the time, Pallas kernels for 0%

profile of v1, /device:TPU:0, one launch (start us, length us, event | category | flops | bytes accessed | tf_op | source)
XLA Modules:
  0.0 431.6 jit_solution(12388343673521004792)
XLA Ops:
  6.5 0.0 copy-start
  6.5 0.0 reduce-scatter.2.cloned.1.call-start
  6.5 0.9 copy.19
  7.4 0.1 eq.42
  7.5 0.1 eq.38
  7.6 0.6 reduce-window.6
  8.2 0.2 slice_reduce_fusion
  8.5 0.1 fusion.10
  8.6 0.1 reduce_sum.21
  8.7 0.1 copy.21
  8.7 0.7 multiply_add_fusion
  9.4 0.1 fusion.7
  9.6 0.0 copy-done
  9.6 2.1 convolution_convert_fusion.1
  11.7 167.7 %all_to_all.15 = bf16[8,64,7168]{2,1,0:T(8,128)(2,1)S(1)} all-to-all(bf16[8,64,7168]{2,1,0:T(8,128)(2,1)S(1)} %bitcast.31), channel_id=1, replica_groups=mesh['rep'=2,'node'=8,'local'=2] {'node'}, dimensions={0} | all-to-all | bytes 14680064 | tf_op jit(solution)/shard_map/all_to_all | solution.py:32
  179.4 0.0 slice-start
  179.4 1.4 pad_maximum_fusion
  180.8 0.0 slice-start.1
  180.8 15.8 %all_to_all.16 = bf16[2,8,64,7168]{3,2,1,0:T(8,128)(2,1)S(1)} all-to-all(bf16[2,8,64,7168]{3,2,1,0:T(8,128)(2,1)S(1)} %pad_maximum_fusion), channel_id=1, replica_groups=mesh['rep'=2,'node'=8,'local'=2] {'local'}, dimensions={0} | all-to-all | bytes 29360128 | tf_op jit(solution)/shard_map/all_to_all | solution.py:30
  196.6 0.0 slice-done
  196.6 0.0 slice-done.1
  196.6 7.7 %fusion.1 = f32[1024,512]{1,0:T(8,128)S(1)} fusion(bf16[1024,7168]{1,0:T(8,128)(2,1)S(1)} %bitcast.34, bf16[1,7168,512]{2,1,0:T(8,128)(2,1)S(1)} %bitcast.37), kind=kOutput, calls=%fused_computation.5 | convolution fusion | flops 7516192768 | bytes 24117248 | tf_op jit(solution)/shard_map/dot_general | solution.py:43
  204.3 10.1 %multiply_convert_fusion = bf16[1024,512]{1,0:T(8,128)(2,1)S(1)} fusion(f32[1024,512]{1,0:T(8,128)S(1)} %fusion.1, bf16[1024,7168]{1,0:T(8,128)(2,1)S(1)} %bitcast.35, bf16[1,7168,512]{2,1,0:T(8,128)(2,1)} %param.9), kind=kOutput, calls=%fused_computation.9 | convolution fusion | flops 7519338496 | bytes 25165824 | tf_op jit(solution)/shard_map/dot_general | solution.py:42
  214.4 14.1 %convolution_convert_fusion = bf16[1024,7168]{1,0:T(8,128)(2,1)} fusion(bf16[1024,512]{1,0:T(8,128)(2,1)S(1)} %multiply_convert_fusion, bf16[1,512,7168]{2,1,0:T(8,128)(2,1)} %param.11), kind=kOutput, calls=%fused_computation.1 | convolution fusion | flops 7523532800 | bytes 23068672 | tf_op jit(solution)/shard_map/dot_general | solution.py:46
  228.5 0.0 reduce-scatter.2.cloned.1.call-update
  228.5 0.0 copy-start.2
  228.5 24.0 %reduce-scatter.2.cloned.1.call-done = bf16[8,64,7168]{2,1,0:T(8,128)(2,1)} async-done(((bf16[16,64,7168]{2,1,0:T(8,128)(2,1)}), bf16[8,64,7168]{2,1,0:T(8,128)(2,1)}) %reduce-scatter.2.cloned.1.call-update) | async-done | bytes 7340048 | tf_op jit(solution)/shard_map/reduce_scatter | solution.py:51
  252.5 5.9 %all-to-all-start.2 = ((bf16[8,64,7168]{2,1,0:T(8,128)(2,1)}), bf16[8,64,7168]{2,1,0:T(8,128)(2,1)}, u32[]{:S(2)}, u32[]{:S(2)}) async-start(bf16[8,64,7168]{2,1,0:T(8,128)(2,1)} %reduce-scatter.2.cloned.1.call-done), calls=%async_computation.3 | async-start | bytes 14680064 | tf_op jit(solution)/shard_map/all_to_all | solution.py:54
  258.4 0.0 copy-done.2
  258.4 0.0 copy-start.1
  258.4 0.1 select_reduce_fusion
  258.6 160.8 %all-to-all-done.2 = bf16[8,64,7168]{2,1,0:T(8,128)(2,1)} async-done(((bf16[8,64,7168]{2,1,0:T(8,128)(2,1)}), bf16[8,64,7168]{2,1,0:T(8,128)(2,1)}, u32[]{:S(2)}, u32[]{:S(2)}) %all-to-all-start.2) | async-done | bytes 7340064 | tf_op jit(solution)/shard_map/all_to_all | solution.py:54
  419.4 5.4 %convolution_convert_fusion.2 = bf16[64,7168]{1,0:T(8,128)(2,1)} fusion(bf16[512,7168]{1,0:T(8,128)(2,1)} %bitcast.9, bf16[64,512]{1,0:T(8,128)(2,1)S(1)} %select_reduce_fusion), kind=kOutput, calls=%fused_computation.3 | convolution fusion | flops 470220800 | bytes 8323072 | tf_op jit(solution)/shard_map/dot_general | solution.py:55
  424.8 0.0 copy-done.1
  (5 shorter events, 0.1 us)
Async XLA Ops:
  6.5 3.1 copy-start
  6.5 245.9 %reduce-scatter.2.cloned.1.call-start = ((), (), s32[]{:S(2)}) async-start(), calls=%async_computation.4 | async-start | bytes 22020096 | tf_op jit(solution)/shard_map/reduce_scatter | solution.py:51
  179.4 17.2 %slice-start = ((s8[7340032]{0:T(1024)(128)(4,1)}), s8[4194304]{0:T(1024)(128)(4,1)S(1)}, s32[]{:S(2)}) async-start(s8[7340032]{0:T(1024)(128)(4,1)} %bitcast.36), calls=%async_computation.5 | async-start | bytes 8388608
  180.8 15.8 %slice-start.1 = ((s8[7340032]{0:T(1024)(128)(4,1)}), s8[3145728]{0:T(1024)(128)(4,1)S(1)}, s32[]{:S(2)}) async-start(s8[7340032]{0:T(1024)(128)(4,1)} %bitcast.36), calls=%async_computation.6 | async-start | bytes 6291456
  228.5 29.9 %copy-start.2 = (bf16[64,4]{0,1:T(4,128)(2,1)S(1)}, bf16[64,4]{0,1:T(4,128)(2,1)}, u32[]{:S(2)}) copy-start(bf16[64,4]{0,1:T(4,128)(2,1)} %param.8) | copy-start | bytes 1540
  252.5 166.9 %all-to-all-start.2 = ((bf16[8,64,7168]{2,1,0:T(8,128)(2,1)}), bf16[8,64,7168]{2,1,0:T(8,128)(2,1)}, u32[]{:S(2)}, u32[]{:S(2)}) async-start(bf16[8,64,7168]{2,1,0:T(8,128)(2,1)} %reduce-scatter.2.cloned.1.call-done), calls=%async_computation.3 | async-start | bytes 14680064 | tf_op jit(solution)/shard_map/all_to_all | solution.py:54
  258.4 166.4 %copy-start.1 = (bf16[64,7168]{1,0:T(8,128)(2,1)S(1)}, bf16[64,7168]{1,0:T(8,128)(2,1)}, u32[]{:S(2)}) copy-start(bf16[64,7168]{1,0:T(8,128)(2,1)} %param.6) | copy-start | bytes 2752516
Sparse Core Ops, SparseCore 0:
  228.6 23.8 reduce-scatter.1
